TPU v7x, 32 devices: a whole 2x2x4 slice. The times are simulated.
32 devices in a mesh: seq: 8 (over z, y), tensor: 4 (over x, core).
Axes of the slice: x: 2, y: 2, z: 4, core: 2. Of those that a mesh axis runs over, the one named last changes fastest.
Arguments:
- residual: bfloat16 [4608, 6144], P('seq', 'tensor'), may hold values from -4 to 4
- queries: bfloat16 [4608, 4096], P(('seq', 'tensor')), may hold values from -6 to 6
- key_rows: bfloat16 [4608, 4096], P(('seq', 'tensor')), may hold values from -6 to 6
- value_rows: bfloat16 [4608, 4096], P(('seq', 'tensor')), may hold values from -6 to 6
- w_out: bfloat16 [4096, 6144], P(None, 'tensor'), may hold values from -0.09375 to 0.09375
- out_gate: float32 [6144], P('tensor'), may hold values from 0.5 to 1.5
- extents: int32 [32, 3], replicated, may hold values from 0 to 1, as said below
Outputs:
- updated: bfloat16 [4608, 6144], P('seq', 'tensor')
Inputs may be any that keep to these rules, and one draw needn't show every extreme that they name: `extents`: reaches in tile-frames are at most 1, in tile-rows at most 1, in tile-columns at most 1; each of these bounds is taken by some head, and some head has reach 0 in tile-rows.
All inputs are finite; a program needn't handle non-finite values.
Results may differ from a plain program's by a relative error of at most 0.0048.
Values may be sent and summed in bfloat16 or wider, within the bound.
A program may use at most 192 MiB of HBM per device.

v0:
```python
import math

import jax
import jax.numpy as jnp
from jax import lax
from jax.sharding import PartitionSpec as P

HEAD_DIM = 128
TILE = 32
HT_DEV = 2
WT = 3


def passed_along(value, axis, by):
    length = lax.axis_size(axis)
    pairs = [(i, i + by) for i in range(length) if 0 <= i + by < length]
    return lax.ppermute(value, axis, pairs)


def tile_coords(row_count, tile_rows, first_row):
    position = jnp.arange(row_count, dtype=jnp.int32)
    frame_id = position // (tile_rows * WT * TILE)
    row_id = first_row + position // (WT * TILE) % tile_rows
    col_id = position // TILE % WT
    return (frame_id, row_id, col_id)


def allowed_keys(query_place, key_place, head_reach, seq_block, seq_count):
    frame_gap = jnp.abs(query_place[0][:, None] - key_place[0][None, :])
    row_gap = jnp.abs(query_place[1][:, None] - key_place[1][None, :])
    col_gap = jnp.abs(query_place[2][:, None] - key_place[2][None, :])
    global_row = key_place[1] + seq_block * HT_DEV
    inside = (global_row >= 0) & (global_row < seq_count * HT_DEV)
    return (
        (frame_gap[None] <= head_reach[:, 0, None, None])
        & (row_gap[None] <= head_reach[:, 1, None, None])
        & (col_gap[None] <= head_reach[:, 2, None, None])
        & inside[None, None, :]
    )


def shards(residual, queries, key_rows, value_rows, w_out, out_gate, extents):
    head_q, head_k, head_v = (
        lax.all_to_all(queries, "tensor", split_axis=1, concat_axis=0, tiled=True),
        lax.all_to_all(key_rows, "tensor", split_axis=1, concat_axis=0, tiled=True),
        lax.all_to_all(value_rows, "tensor", split_axis=1, concat_axis=0, tiled=True),
    )
    tokens = head_q.shape[0]
    inner_dev = head_q.shape[1]
    head_dim = HEAD_DIM
    heads_here = inner_dev // head_dim
    seq_block = lax.axis_index("seq")
    seq_count = lax.axis_size("seq")
    head_reach = lax.dynamic_slice_in_dim(
        extents, lax.axis_index("tensor") * heads_here, heads_here, 0
    )
    query_tiles = head_q.reshape(tokens, heads_here, head_dim)
    query_place = tile_coords(tokens, HT_DEV, 0)
    stacked = jnp.stack([head_k, head_v])

    def part_scores(pair_rows, key_place):
        key_tiles = pair_rows[0].reshape(-1, heads_here, head_dim)
        scores = jnp.einsum(
            "qhd,khd->hqk", query_tiles, key_tiles, preferred_element_type=jnp.float32
        ) / math.sqrt(head_dim)
        allowed = allowed_keys(query_place, key_place, head_reach, seq_block, seq_count)
        return jnp.where(allowed, scores, -1e30)

    lower_part = passed_along(stacked, "seq", 1)
    upper_part = passed_along(stacked, "seq", -1)
    remote = [
        (lower_part, tile_coords(tokens, HT_DEV, -HT_DEV)),
        (upper_part, tile_coords(tokens, HT_DEV, HT_DEV)),
    ]
    own_scores = part_scores(stacked, query_place)
    scores = jnp.concatenate(
        [own_scores] + [part_scores(pair_rows, key_place) for pair_rows, key_place in remote],
        axis=-1,
    )
    value_all = jnp.concatenate(
        [stacked[1]] + [pair_rows[1] for pair_rows, key_place in remote], axis=0
    )
    row_max = jnp.max(scores, axis=-1, keepdims=True)
    exp_scores = jnp.exp(scores - row_max)
    row_sum = jnp.sum(exp_scores, axis=-1, keepdims=True)
    weights = (exp_scores / row_sum).astype(jnp.bfloat16)
    attended = jnp.einsum(
        "hqk,khd->qhd",
        weights,
        value_all.reshape(-1, heads_here, head_dim),
        preferred_element_type=jnp.float32,
    )
    head_out = attended.reshape(tokens, inner_dev).astype(jnp.bfloat16)
    projected = jnp.dot(
        lax.all_gather(head_out, "tensor", axis=1, tiled=True),
        w_out,
        preferred_element_type=jnp.float32,
    )
    return (residual.astype(jnp.float32) + out_gate * projected).astype(jnp.bfloat16)


def solution(mesh):
    placed = (
        P("seq", "tensor"),
        P(("seq", "tensor"), None),
        P(("seq", "tensor"), None),
        P(("seq", "tensor"), None),
        P(None, "tensor"),
        P("tensor"),
        P(),
    )
    return jax.shard_map(
        shards, mesh=mesh, in_specs=placed, out_specs=P("seq", "tensor"), check_vma=False
    )
```

profile of v0, /device:TPU:9, one launch (start us, length us, event | category | flops | bytes accessed | tf_op | source)
XLA Modules:
  0.0 308.5 jit_solution(9259472700142970301)
XLA Ops:
  6.5 2.5 copy.92
  9.1 4.2 %all-to-all-start.1 = ((bf16[144,4,1024]{2,0,1:T(8,128)(2,1)}), bf16[144,4,1024]{2,0,1:T(8,128)(2,1)S(1)}, u32[]{:S(2)}, u32[]{:S(2)}) async-start(bf16[144,4,1024]{2,0,1:T(8,128)(2,1)} %bitcast.60), calls=%async_computation.1 | async-start | bytes 2359296 | tf_op jit(solution)/shard_map/all_to_all | solution.py:45
  14.3 13.9 %all-to-all-done.1 = bf16[144,4,1024]{2,0,1:T(8,128)(2,1)S(1)} async-done(((bf16[144,4,1024]{2,0,1:T(8,128)(2,1)}), bf16[144,4,1024]{2,0,1:T(8,128)(2,1)S(1)}, u32[]{:S(2)}, u32[]{:S(2)}) %all-to-all-start.1) | async-done | bytes 1179680 | tf_op jit(solution)/shard_map/all_to_all | solution.py:45
  28.2 4.4 %all-to-all-start = ((bf16[144,4,1024]{2,0,1:T(8,128)(2,1)}), bf16[144,4,1024]{2,0,1:T(8,128)(2,1)S(1)}, u32[]{:S(2)}, u32[]{:S(2)}) async-start(bf16[144,4,1024]{2,0,1:T(8,128)(2,1)} %bitcast.59), calls=%async_computation | async-start | bytes 2359296 | tf_op jit(solution)/shard_map/all_to_all | solution.py:46
  33.8 13.8 %all-to-all-done = bf16[144,4,1024]{2,0,1:T(8,128)(2,1)S(1)} async-done(((bf16[144,4,1024]{2,0,1:T(8,128)(2,1)}), bf16[144,4,1024]{2,0,1:T(8,128)(2,1)S(1)}, u32[]{:S(2)}, u32[]{:S(2)}) %all-to-all-start) | async-done | bytes 1179680 | tf_op jit(solution)/shard_map/all_to_all | solution.py:46
  47.6 4.4 %all-to-all-start.2 = ((bf16[144,4,1024]{2,0,1:T(8,128)(2,1)}), bf16[144,4,1024]{2,0,1:T(8,128)(2,1)S(1)}, u32[]{:S(2)}, u32[]{:S(2)}) async-start(bf16[144,4,1024]{2,0,1:T(8,128)(2,1)} %bitcast.61), calls=%async_computation.2 | async-start | bytes 2359296 | tf_op jit(solution)/shard_map/all_to_all | solution.py:44
  52.0 1.6 pad_maximum_fusion
  53.6 3.0 collective-permute-start.1
  57.3 2.2 collective-permute-start
  60.8 2.0 subtract_abs_fusion.2
  62.8 2.7 subtract_abs_fusion
  65.6 1.5 all-to-all-done.2
  70.0 8.3 %fusion.36 = (f32[8,576]{1,0:T(8,128)S(1)}, f32[8,576,576]{2,1,0:T(8,128)}) fusion(bf16[576,8,128]{2,1,0:T(8,128)(2,1)S(1)} %bitcast.79, bf16[576,8,128]{2,1,0:T(8,128)(2,1)S(1)} %bitcast.74, pred[576]{0:T(1024)(128)(4,1)S(1)} %copy-done.17, s32[8]{0:T(128)S(1)} %copy-done.13, s32[576,576]{1,0:T(8,128)S(1)} %copy-done.2, s32[8]{0:T(128)S(1)} %get-tuple-element.12, ...), kind=kOutput, calls=%fused_computation.83 | convolution fusion | flops 703360512 | bytes 16976544 | tf_op jit(solution)/shard_map/qhd,khd->hqk/dot_general | solution.py:63
  78.3 80.9 %collective-permute-done.1 = bf16[2,576,1024]{2,1,0:T(8,128)(2,1)} collective-permute-done((bf16[2,576,1024]{2,1,0:T(8,128)(2,1)}, bf16[2,576,1024]{2,1,0:T(8,128)(2,1)}, u32[]{:S(2)}, u32[]{:S(2)}) %collective-permute-start.1) | collective-permute-done | bytes 2359328 | tf_op jit(solution)/shard_map/ppermute | solution.py:17
  159.2 2.1 slice_bitcast_fusion.2
  162.1 2.1 slice_bitcast_fusion.3
  165.9 8.1 %fusion.35 = (f32[8,576]{1,0:T(8,128)S(1)}, f32[8,576,576]{2,1,0:T(8,128)}) fusion(bf16[576,8,128]{2,1,0:T(8,128)(2,1)S(1)} %bitcast.75, bf16[576,8,128]{2,1,0:T(8,128)(2,1)S(1)} %bitcast.77, pred[576]{0:T(1024)(128)(4,1)S(1)} %copy-done.10, s32[8]{0:T(128)S(1)} %copy-done.13, s32[576,576]{1,0:T(8,128)S(1)} %copy-done.2, s32[8]{0:T(128)S(1)} %copy-done.12, ...), kind=kOutput, calls=%fused_computation.82 | convolution fusion | flops 703360512 | bytes 16976544 | tf_op jit(solution)/shard_map/qhd,khd->hqk/dot_general | solution.py:63
  174.0 8.1 %fusion.37 = (f32[8,576]{1,0:T(8,128)S(1)}, f32[8,576,576]{2,1,0:T(8,128)}) fusion(bf16[576,8,128]{2,1,0:T(8,128)(2,1)S(1)} %bitcast.76, bf16[576,8,128]{2,1,0:T(8,128)(2,1)S(1)} %bitcast.78, pred[576]{0:T(1024)(128)(4,1)S(1)} %copy-done.9, s32[8]{0:T(128)S(1)} %copy-done.13, s32[576,576]{1,0:T(8,128)S(1)} %copy-done.2, s32[8]{0:T(128)S(1)} %copy-done.12, ...), kind=kOutput, calls=%fused_computation.84 | convolution fusion | flops 703360512 | bytes 16976544 | tf_op jit(solution)/shard_map/qhd,khd->hqk/dot_general | solution.py:63
  182.7 36.3 %concatenate.17 = f32[8,576,1728]{2,1,0:T(8,128)} concatenate(f32[8,576,576]{2,1,0:T(8,128)} %get-tuple-element.18, f32[8,576,576]{2,1,0:T(8,128)} %get-tuple-element.20, f32[8,576,576]{2,1,0:T(8,128)} %get-tuple-element.16), dimensions={2} | concatenate | bytes 63700992 | tf_op jit(solution)/shard_map/concatenate | solution.py:76
  219.1 14.1 %fusion = f32[8,576]{1,0:T(8,128)} fusion(f32[8,576,1728]{2,1,0:T(8,128)} %concatenate.17, f32[8,576]{1,0:T(8,128)} %maximum_maximum_fusion), kind=kLoop, calls=%fused_computation.2 | loop fusion | flops 15920640 | bytes 31887360 | tf_op jit(solution)/shard_map/reduce_sum | solution.py:85
  233.2 14.3 %fusion.13 = bf16[8,72,8,128]{3,2,1,0:T(8,128)(2,1)} fusion(bf16[576,8,128]{2,0,1:T(8,128)(2,1)S(1)} %copy.41, bf16[576,8,128]{2,0,1:T(8,128)(2,1)S(1)} %copy.40, bf16[576,8,128]{2,0,1:T(8,128)(2,1)S(1)} %copy.39, f32[8,576,1728]{2,1,0:T(8,128)} %concatenate.17, f32[8,576]{1,0:T(8,128)} %fusion, f32[8,576]{1,0:T(8,128)} %maximum_maximum_fusion), kind=kOutput, calls=%fused_computation.30 | convolution fusion | flops 2073526272 | bytes 36605952 | tf_op jit(solution)/shard_map/hqk,khd->qhd/dot_general | solution.py:87
  247.5 2.8 copy.90
  250.3 38.6 %all-gather.2.cloned.1.call-done = bf16[576,4096]{1,0:T(8,128)(2,1)} async-done(((bf16[576,1024]{1,0:T(8,128)(2,1)}), bf16[576,4096]{1,0:T(8,128)(2,1)}) %all-gather.2.cloned.1.call-update) | async-done | bytes 4718608 | tf_op jit(solution)/shard_map/all_gather | solution.py:95
  288.9 12.7 %add_convert_fusion = bf16[576,1536]{1,0:T(8,128)(2,1)} fusion(bf16[576,1536]{1,0:T(8,128)(2,1)S(1)} %copy-done.15, bf16[576,4096]{1,0:T(8,128)(2,1)} %all-gather.2.cloned.1.call-done, bf16[4096,1536]{1,0:T(8,128)(2,1)} %param.11, f32[1536]{0:T(1024)S(1)} %copy-done.16), kind=kOutput, calls=%fused_computation.22 | convolution fusion | flops 7251296256 | bytes 20846592 | tf_op jit(solution)/shard_map/dot_general | solution.py:94
  (60 shorter events, 10.1 us)
Async XLA Ops:
  6.5 53.0 %copy-start = (s32[32,3]{0,1:T(4,128)S(1)}, s32[32,3]{0,1:T(4,128)}, u32[]{:S(2)}) copy-start(s32[32,3]{0,1:T(4,128)} %param.13) | copy-start | bytes 1156
  6.5 6.7 %copy-start.7 = (bf16[144,4096]{1,0:T(8,128)(2,1)S(1)}, bf16[144,4096]{1,0:T(8,128)(2,1)}, u32[]{:S(2)}) copy-start(bf16[144,4096]{1,0:T(8,128)(2,1)} %param.10) | copy-start | bytes 3538948
  9.1 19.2 %all-to-all-start.1 = ((bf16[144,4,1024]{2,0,1:T(8,128)(2,1)}), bf16[144,4,1024]{2,0,1:T(8,128)(2,1)S(1)}, u32[]{:S(2)}, u32[]{:S(2)}) async-start(bf16[144,4,1024]{2,0,1:T(8,128)(2,1)} %bitcast.60), calls=%async_computation.1 | async-start | bytes 2359296 | tf_op jit(solution)/shard_map/all_to_all | solution.py:45
  13.2 19.4 %copy-start.8 = (bf16[144,4096]{1,0:T(8,128)(2,1)S(1)}, bf16[144,4096]{1,0:T(8,128)(2,1)}, u32[]{:S(2)}) copy-start(bf16[144,4096]{1,0:T(8,128)(2,1)} %param.8) | copy-start | bytes 3538948
  28.2 19.4 %all-to-all-start = ((bf16[144,4,1024]{2,0,1:T(8,128)(2,1)}), bf16[144,4,1024]{2,0,1:T(8,128)(2,1)S(1)}, u32[]{:S(2)}, u32[]{:S(2)}) async-start(bf16[144,4,1024]{2,0,1:T(8,128)(2,1)} %bitcast.59), calls=%async_computation | async-start | bytes 2359296 | tf_op jit(solution)/shard_map/all_to_all | solution.py:46
  47.6 19.5 %all-to-all-start.2 = ((bf16[144,4,1024]{2,0,1:T(8,128)(2,1)}), bf16[144,4,1024]{2,0,1:T(8,128)(2,1)S(1)}, u32[]{:S(2)}, u32[]{:S(2)}) async-start(bf16[144,4,1024]{2,0,1:T(8,128)(2,1)} %bitcast.61), calls=%async_computation.2 | async-start | bytes 2359296 | tf_op jit(solution)/shard_map/all_to_all | solution.py:44
  52.0 236.9 %all-gather.2.cloned.1.call-start = ((), (), s32[]{:S(2)}) async-start(), calls=%async_computation.3 | async-start | bytes 5898240 | tf_op jit(solution)/shard_map/all_gather | solution.py:95
  53.6 105.6 %collective-permute-start.1 = (bf16[2,576,1024]{2,1,0:T(8,128)(2,1)}, bf16[2,576,1024]{2,1,0:T(8,128)(2,1)}, u32[]{:S(2)}, u32[]{:S(2)}) collective-permute-start(bf16[2,576,1024]{2,1,0:T(8,128)(2,1)} %pad_maximum_fusion), channel_id=1, source_target_pairs={{4,0},{8,4},{12,8},{16,12},{20,16},{24,20},{28,24},{5,1},{9,5},{13... | collective-permute-start | bytes 7077896 | tf_op jit(solution)/shard_map/ppermute | solution.py:17
  57.3 104.8 %collective-permute-start = (bf16[2,576,1024]{2,1,0:T(8,128)(2,1)}, bf16[2,576,1024]{2,1,0:T(8,128)(2,1)}, u32[]{:S(2)}, u32[]{:S(2)}) collective-permute-start(bf16[2,576,1024]{2,1,0:T(8,128)(2,1)} %pad_maximum_fusion), channel_id=1, source_target_pairs={{0,4},{4,8},{8,12},{12,16},{16,20},{20,24},{24,28},{1,5},{5,9},{9,... | collective-permute-start | bytes 7077896 | tf_op jit(solution)/shard_map/ppermute | solution.py:17
  60.8 7.5 %copy-start.11 = (s32[8]{0:T(128)}, s32[8]{0:T(128)S(1)}, u32[]{:S(2)}) copy-start(s32[8]{0:T(128)S(1)} %get-tuple-element.12) | copy-start | bytes 100
  67.7 1.4 copy-start.2
  67.7 1.8 copy-start.3
  67.8 2.2 copy-start.6
  67.8 2.2 copy-start.13
  67.8 2.2 copy-start.14
  67.8 2.2 copy-start.17
  164.6 1.4 copy-start.5
  164.6 1.4 copy-start.10
  164.6 1.4 copy-start.12
  165.9 8.1 %copy-start.4 = (s32[576,576]{1,0:T(8,128)S(1)}, s32[576,576]{1,0:T(8,128)}, u32[]{:S(2)}) copy-start(s32[576,576]{1,0:T(8,128)} %get-tuple-element.11) | copy-start | bytes 3981316
  165.9 8.1 %copy-start.9 = (pred[576]{0:T(1024)(128)(4,1)S(1)}, pred[576]{0:T(1024)(128)(4,1)}, u32[]{:S(2)}) copy-start(pred[576]{0:T(1024)(128)(4,1)} %get-tuple-element.22) | copy-start | bytes 1732
  247.5 41.4 %copy-start.15 = (bf16[576,1536]{1,0:T(8,128)(2,1)S(1)}, bf16[576,1536]{1,0:T(8,128)(2,1)}, u32[]{:S(2)}) copy-start(bf16[576,1536]{1,0:T(8,128)(2,1)} %param.7) | copy-start | bytes 5308420
  247.5 41.4 %copy-start.16 = (f32[1536]{0:T(1024)S(1)}, f32[1536]{0:T(1024)}, u32[]{:S(2)}) copy-start(f32[1536]{0:T(1024)} %param.12) | copy-start | bytes 18436
  288.9 12.7 %copy-start.1 = (s32[32,3]{0,1:T(4,128)S(1)}, s32[32,3]{0,1:T(4,128)}, u32[]{:S(2)}) copy-start(s32[32,3]{0,1:T(4,128)} %param.13) | copy-start | bytes 1156
Sparse Core Ops, SparseCore 0:
  250.4 38.4 all-gather.1
where the time goes:
time: 311 us; the launch traced here: 308 us
  waiting for transfers between devices  149 us (48%)
  local copies, waits for them, and re-layouts  54.1 us (17%)
  matrix products  51.5 us (17%)
  other arithmetic  22.3 us (7%)
  starting transfers between devices  18.2 us (6%)
  between operations  13.6 us (4%)
    ppermute x2, waiting for transfers between devices, passed_along(): return lax.ppermute(value, axis, pairs)  80.9 us
    all_gather x1, waiting for transfers between devices, shards(): lax.all_gather(head_out, 'tensor', axis=1, tiled=True)  38.6 us
    concatenate x1, local copies, waits for them, and re-layouts, shards(): jnp.concatenate([own_scores] + [part_scores(pair_rows, key_place) for pai...  36.3 us
    dot_general x3, matrix products, part_scores(): jnp.einsum('qhd,khd->hqk', query_tiles, key_tiles, preferred_element_type...  24.5 us
    dot_general x1, matrix products, shards(): jnp.einsum('hqk,khd->qhd', weights, value_all.reshape(-1, heads_here, hea...  14.3 us
    reduce_sum x1, other arithmetic, shards(): row_sum = jnp.sum(exp_scores, axis=-1, keepdims=True)  14.1 us
    all_to_all x1, waiting for transfers between devices, shards(): lax.all_to_all(key_rows, 'tensor', split_axis=1, concat_axis=0, tiled=True)  13.9 us
    all_to_all x1, waiting for transfers between devices, shards(): lax.all_to_all(value_rows, 'tensor', split_axis=1, concat_axis=0, tiled=T...  13.8 us
  transfers between devices with their start and end apart: 6, of which 5 were waited for; matrix products, arithmetic and copies ran while one was open for 7% of the time, Pallas kernels for 0%

commit v1 on v0

v1 whole, which is shorter than its diff:
```python
import functools
import math

import jax
import jax.numpy as jnp
import numpy as np
from jax import lax
from jax.experimental import pallas as pl
from jax.experimental.pallas import tpu as pltpu
from jax.sharding import PartitionSpec as P

HEAD_DIM = 128
TILE = 32
HT_DEV = 2
WT = 3
CHUNK_HEADS = 2
FAR = -1e30
MESH = pl.DeviceIdType.MESH


def passed_along(value, axis, by):
    length = lax.axis_size(axis)
    pairs = [(i, i + by) for i in range(length) if 0 <= i + by < length]
    return lax.ppermute(value, axis, pairs)


def tile_coords(row_count, tile_rows, first_row):
    position = jnp.arange(row_count, dtype=jnp.int32)
    frame_id = position // (tile_rows * WT * TILE)
    row_id = first_row + position // (WT * TILE) % tile_rows
    col_id = position // TILE % WT
    return (frame_id, row_id, col_id)


def allowed_keys(query_place, key_place, head_reach, seq_block, seq_count):
    frame_gap = jnp.abs(query_place[0][:, None] - key_place[0][None, :])
    row_gap = jnp.abs(query_place[1][:, None] - key_place[1][None, :])
    col_gap = jnp.abs(query_place[2][:, None] - key_place[2][None, :])
    global_row = key_place[1] + seq_block * HT_DEV
    inside = (global_row >= 0) & (global_row < seq_count * HT_DEV)
    return (
        (frame_gap[None] <= head_reach[:, 0, None, None])
        & (row_gap[None] <= head_reach[:, 1, None, None])
        & (col_gap[None] <= head_reach[:, 2, None, None])
        & inside[None, None, :]
    )


def plain_shards(residual, queries, key_rows, value_rows, w_out, out_gate, extents):
    head_q, head_k, head_v = (
        lax.all_to_all(queries, "tensor", split_axis=1, concat_axis=0, tiled=True),
        lax.all_to_all(key_rows, "tensor", split_axis=1, concat_axis=0, tiled=True),
        lax.all_to_all(value_rows, "tensor", split_axis=1, concat_axis=0, tiled=True),
    )
    tokens, inner_dev = head_q.shape
    heads_here = inner_dev // HEAD_DIM
    seq_block = lax.axis_index("seq")
    seq_count = lax.axis_size("seq")
    head_reach = lax.dynamic_slice_in_dim(
        extents, lax.axis_index("tensor") * heads_here, heads_here, 0
    )
    query_tiles = head_q.reshape(tokens, heads_here, HEAD_DIM)
    query_place = tile_coords(tokens, HT_DEV, 0)
    stacked = jnp.stack([head_k, head_v])

    def part_scores(pair_rows, key_place):
        key_tiles = pair_rows[0].reshape(-1, heads_here, HEAD_DIM)
        scores = jnp.einsum(
            "qhd,khd->hqk", query_tiles, key_tiles, preferred_element_type=jnp.float32
        ) / math.sqrt(HEAD_DIM)
        allowed = allowed_keys(query_place, key_place, head_reach, seq_block, seq_count)
        return jnp.where(allowed, scores, FAR)

    by_row = stacked.reshape(2, -1, HT_DEV, WT * TILE, inner_dev)
    halves = tokens // HT_DEV
    last_row = by_row[:, :, HT_DEV - 1].reshape(2, halves, inner_dev)
    first_row = by_row[:, :, 0].reshape(2, halves, inner_dev)
    parts = [
        (stacked, query_place),
        (passed_along(last_row, "seq", 1), tile_coords(halves, 1, -1)),
        (passed_along(first_row, "seq", -1), tile_coords(halves, 1, HT_DEV)),
    ]
    scores = jnp.concatenate([part_scores(*part) for part in parts], axis=-1)
    value_all = jnp.concatenate([pair_rows[1] for pair_rows, _ in parts], axis=0)
    row_max = jnp.max(scores, axis=-1, keepdims=True)
    exp_scores = jnp.exp(scores - row_max)
    row_sum = jnp.sum(exp_scores, axis=-1, keepdims=True)
    weights = (exp_scores / row_sum).astype(jnp.bfloat16)
    attended = jnp.einsum(
        "hqk,khd->qhd",
        weights,
        value_all.reshape(-1, heads_here, HEAD_DIM),
        preferred_element_type=jnp.float32,
    )
    head_out = attended.reshape(tokens, inner_dev).astype(jnp.bfloat16)
    projected = jnp.dot(
        lax.all_gather(head_out, "tensor", axis=1, tiled=True),
        w_out,
        preferred_element_type=jnp.float32,
    )
    return (residual.astype(jnp.float32) + out_gate * projected).astype(jnp.bfloat16)


def mask_features(frames):
    span = WT * TILE
    q_feat = np.zeros((2, frames * span, HEAD_DIM), np.float32)
    k_feat = np.zeros((2, frames * 3 * span, HEAD_DIM), np.float32)
    q_at = np.arange(frames * span)
    q_frame, q_col = q_at // span, q_at // TILE % WT
    k_at = np.arange(frames * 3 * span)
    k_frame, k_col = k_at // (3 * span), k_at // TILE % WT
    k_row = k_at // span % 3 - 1
    for r in range(2):
        for j in range(3):
            q_feat[r, :, j] = q_feat[r, :, 8 + j] = q_frame == j
            q_feat[r, :, 3 + j] = q_feat[r, :, 11 + j] = q_col == j
            k_feat[r, :, j] = FAR * (abs(k_frame - j) >= 2)
            k_feat[r, :, 8 + j] = FAR * (abs(k_frame - j) == 1)
            k_feat[r, :, 3 + j] = FAR * (abs(k_col - j) >= 2)
            k_feat[r, :, 11 + j] = FAR * (abs(k_col - j) == 1)
        q_feat[r, :, 14:17] = 1.0
        k_feat[r, :, 14] = FAR * (k_row != 0)
    k_feat[0, :, 15] = FAR * (k_row == -1)
    k_feat[1, :, 16] = FAR * (k_row == 1)
    return jnp.asarray(q_feat, jnp.bfloat16), jnp.asarray(k_feat, jnp.bfloat16)


def kernel(
    n_t, n_s, frames, q_hbm, k_hbm, v_hbm, w_hbm, res_hbm, gate_ref, coef_ref, qf_ref, kf_ref,
    out_ref, own, halo, gat, wbuf, res, acc,
    a_send, a_recv, a_loc, h_send, h_recv, g_send, g_recv, w_sem, r_sem,
):
    rows = q_hbm.shape[0]
    inner_dev = q_hbm.shape[1] // n_t
    width = CHUNK_HEADS * HEAD_DIM
    chunks = inner_dev // width
    span = WT * TILE
    me, sb = lax.axis_index("tensor"), lax.axis_index("seq")
    mate = me // 2 * 2 + 1 - lax.rem(me, 2)
    across = lax.rem(me + n_t // 2, n_t)
    srcs = (k_hbm, v_hbm, q_hbm)
    has_up, has_down = sb < n_s - 1, sb > 0

    barrier = pltpu.get_barrier_semaphore()
    for d in range(1, n_t):
        pl.semaphore_signal(
            barrier, inc=1, device_id={"tensor": lax.rem(me + d, n_t)}, device_id_type=MESH
        )

    @pl.when(has_up)
    def _():
        pl.semaphore_signal(barrier, inc=1, device_id={"seq": sb + 1}, device_id_type=MESH)

    @pl.when(has_down)
    def _():
        pl.semaphore_signal(barrier, inc=1, device_id={"seq": sb - 1}, device_id_type=MESH)

    inner_block = has_up & has_down

    @pl.when(inner_block)
    def _():
        pl.semaphore_wait(barrier, n_t + 1)

    @pl.when(jnp.logical_not(inner_block))
    def _():
        pl.semaphore_wait(barrier, n_t)

    def columns(owner, c):
        return pl.ds(pl.multiple_of(owner * inner_dev + c * width, width), width)

    def slot(owner):
        return pl.ds(pl.multiple_of(owner * rows, 16), rows)

    def sent(a, c, d, owner):
        peer = lax.rem(me + d, n_t)
        return pltpu.make_async_remote_copy(
            src_ref=srcs[a].at[:, columns(peer, c)],
            dst_ref=own.at[a, c, slot(owner), :],
            send_sem=a_send.at[a, c, d - 1],
            recv_sem=a_recv.at[a, c, d - 1],
            device_id={"tensor": peer},
            device_id_type=MESH,
        )

    def kept(a, c):
        return pltpu.make_async_copy(
            srcs[a].at[:, columns(me, c)], own.at[a, c, slot(me), :], a_loc.at[a, c]
        )

    def arrived(a, c):
        for d in range(1, n_t):
            sent(a, c, d, lax.rem(me - d + n_t, n_t)).wait_recv()
        kept(a, c).wait()

    def edge(way, a, c, f):
        first = f * 2 * span + (span if way == 0 else 0)
        return pltpu.make_async_remote_copy(
            src_ref=own.at[a, c, pl.ds(first, span), :],
            dst_ref=halo.at[way, a, c, pl.ds(f * span, span), :],
            send_sem=h_send.at[way, a, c, f],
            recv_sem=h_recv.at[way, a, c, f],
            device_id={"seq": sb + 1 if way == 0 else sb - 1},
            device_id_type=MESH,
        )

    def shared(c, kind):
        piece = across if kind == 2 else me
        return pltpu.make_async_remote_copy(
            src_ref=gat.at[c, piece],
            dst_ref=gat.at[c, piece],
            send_sem=g_send.at[c, kind],
            recv_sem=g_recv.at[c, kind],
            device_id={"tensor": across if kind == 1 else mate},
            device_id_type=MESH,
        )

    def shared_in(c, kind):
        piece = (mate, across, lax.rem(mate + n_t // 2, n_t))[kind]
        return pltpu.make_async_remote_copy(
            src_ref=gat.at[c, piece],
            dst_ref=gat.at[c, piece],
            send_sem=g_send.at[c, kind],
            recv_sem=g_recv.at[c, kind],
            device_id={"tensor": across if kind == 1 else mate},
            device_id_type=MESH,
        )

    def weights_in(c, s):
        return pltpu.make_async_copy(
            w_hbm.at[pl.ds(pl.multiple_of(s * inner_dev + c * width, width), width), :],
            wbuf.at[c, pl.ds(s * width, width), :],
            w_sem.at[c, s],
        )

    @pl.loop(0, chunks)
    def _(c):
        for a in range(3):
            for d in (2, 1, 3):
                sent(a, c, d, me).start()
            kept(a, c).start()

    @pl.loop(0, chunks)
    def _(c):
        for s in range(n_t):
            weights_in(c, s).start()

    res_copy = pltpu.make_async_copy(res_hbm, res, r_sem)
    res_copy.start()
    acc[...] = jnp.zeros_like(acc)

    @pl.when(sb == 0)
    def _():
        halo[0] = jnp.zeros(halo.shape[1:], halo.dtype)

    @pl.when(sb == n_s - 1)
    def _():
        halo[1] = jnp.zeros(halo.shape[1:], halo.dtype)

    def halo_start(c):
        for a in range(2):
            arrived(a, c)

            @pl.when(has_up)
            def _():
                for f in range(frames):
                    edge(0, a, c, f).start()

            @pl.when(has_down)
            def _():
                for f in range(frames):
                    edge(1, a, c, f).start()

    def gathered(a, c, r, lanes):
        parts = []
        for f in range(frames):
            near = own[a, c, f * 2 * span : (f + 1) * 2 * span, lanes]
            far = halo[r, a, c, f * span : (f + 1) * span, lanes]
            parts += [far, near] if r == 0 else [near, far]
        return jnp.concatenate(parts, axis=0)

    def attend(c):
        arrived(2, c)
        for a in range(2):

            @pl.when(has_down)
            def _():
                for f in range(frames):
                    edge(0, a, c, f).wait_recv()

            @pl.when(has_up)
            def _():
                for f in range(frames):
                    edge(1, a, c, f).wait_recv()

        ones = jnp.ones((frames * 3 * span, HEAD_DIM), jnp.bfloat16)
        for h in range(CHUNK_HEADS):
            lanes = slice(h * HEAD_DIM, (h + 1) * HEAD_DIM)
            coef = coef_ref[c * CHUNK_HEADS + h]
            for r in range(2):
                q_part = jnp.concatenate(
                    [own[2, c, (2 * f + r) * span : (2 * f + r + 1) * span, lanes]
                     for f in range(frames)], axis=0)
                q_feat = (qf_ref[r].astype(jnp.float32) * coef).astype(jnp.bfloat16)
                scores = lax.dot_general(
                    jnp.concatenate([q_part, q_feat], axis=1),
                    jnp.concatenate([gathered(0, c, r, lanes), kf_ref[r]], axis=1),
                    (((1,), (1,)), ((), ())),
                    preferred_element_type=jnp.float32,
                )
                top = jnp.max(scores, axis=-1, keepdims=True)
                weights = jnp.exp2(
                    (scores - top) * (math.log2(math.e) / math.sqrt(HEAD_DIM))
                ).astype(jnp.bfloat16)
                both = jnp.dot(
                    weights,
                    jnp.concatenate([gathered(1, c, r, lanes), ones], axis=1),
                    preferred_element_type=jnp.float32,
                )
                done = (both[:, :HEAD_DIM] / both[:, HEAD_DIM:]).astype(jnp.bfloat16)
                for f in range(frames):
                    gat[c, me, (2 * f + r) * span : (2 * f + r + 1) * span, lanes] = done[
                        f * span : (f + 1) * span
                    ]
        shared(c, 1).start()
        shared(c, 0).start()

    n_tile = 512

    def project(c):
        shared_in(c, 0).wait_recv()
        shared_in(c, 2).wait_recv()
        for s in range(n_t):
            weights_in(c, s).wait()

        @pl.loop(0, acc.shape[1] // n_tile)
        def _(j):
            cols = pl.ds(pl.multiple_of(j * n_tile, n_tile), n_tile)
            lhs = jnp.concatenate([gat[c, s] for s in range(n_t)], axis=1)
            acc[:, cols] += jnp.dot(lhs, wbuf[c, :, cols], preferred_element_type=jnp.float32)

    halo_start(0)

    @pl.loop(0, chunks + 2)
    def _(s):
        @pl.when(s + 1 < chunks)
        def _():
            halo_start(s + 1)

        @pl.when(s >= 2)
        def _():
            project(s - 2)

        @pl.when((s >= 1) & (s <= chunks))
        def _():
            shared_in(s - 1, 1).wait_recv()
            shared(s - 1, 2).start()

        @pl.when(s < chunks)
        def _():
            attend(s)

    res_copy.wait()
    out_ref[...] = (res[...].astype(jnp.float32) + gate_ref[...] * acc[...]).astype(out_ref.dtype)

    @pl.loop(0, chunks)
    def _(c):
        for a in range(3):
            for d in range(1, n_t):
                sent(a, c, d, me).wait_send()
        for a in range(2):

            @pl.when(has_up)
            def _():
                for f in range(frames):
                    edge(0, a, c, f).wait_send()

            @pl.when(has_down)
            def _():
                for f in range(frames):
                    edge(1, a, c, f).wait_send()

        for kind in range(3):
            shared(c, kind).wait_send()


def shards(residual, queries, key_rows, value_rows, w_out, out_gate, extents):
    n_t, n_s = lax.axis_size("tensor"), lax.axis_size("seq")
    rows, inner = queries.shape
    tokens, out_cols = residual.shape
    inner_dev = inner // n_t
    width = CHUNK_HEADS * HEAD_DIM
    if n_t != 4 or n_s < 2 or rows % 16 or inner_dev % width or out_cols % 512:
        return plain_shards(
            residual, queries, key_rows, value_rows, w_out, out_gate, extents
        )
    heads_here = inner_dev // HEAD_DIM
    chunks = inner_dev // width
    frames = tokens // (HT_DEV * WT * TILE)
    half = tokens // HT_DEV
    reach = lax.dynamic_slice_in_dim(extents, lax.axis_index("tensor") * heads_here, heads_here, 0)
    stops = (reach < 1).astype(jnp.float32)
    sb = lax.axis_index("seq")
    at_edge = jnp.stack([sb == 0, sb == n_s - 1]).astype(jnp.float32)
    coef = jnp.concatenate(
        [
            jnp.ones((heads_here, 8), jnp.float32),
            jnp.repeat(stops[:, 0:1], 3, axis=1),
            jnp.repeat(stops[:, 2:3], 3, axis=1),
            stops[:, 1:2],
            jnp.broadcast_to(at_edge[None], (heads_here, 2)),
            jnp.zeros((heads_here, HEAD_DIM - 17), jnp.float32),
        ],
        axis=1,
    ).reshape(heads_here, 1, HEAD_DIM)
    q_feat, k_feat = mask_features(frames)
    hbm = pl.BlockSpec(memory_space=pl.ANY)
    vmem = pl.BlockSpec(memory_space=pltpu.VMEM)
    dma = pltpu.SemaphoreType.DMA
    bf16 = jnp.bfloat16
    return pl.pallas_call(
        functools.partial(kernel, n_t, n_s, frames),
        out_shape=jax.ShapeDtypeStruct((tokens, out_cols), bf16),
        in_specs=[hbm] * 5 + [vmem] * 4,
        out_specs=vmem,
        scratch_shapes=[
            pltpu.VMEM((3, chunks, tokens, width), bf16),
            pltpu.VMEM((2, 2, chunks, half, width), bf16),
            pltpu.VMEM((chunks, n_t, tokens, width), bf16),
            pltpu.VMEM((chunks, n_t * width, out_cols), bf16),
            pltpu.VMEM((tokens, out_cols), bf16),
            pltpu.VMEM((tokens, out_cols), jnp.float32),
            dma((3, chunks, n_t - 1)),
            dma((3, chunks, n_t - 1)),
            dma((3, chunks)),
            dma((2, 2, chunks, frames)),
            dma((2, 2, chunks, frames)),
            dma((chunks, 3)),
            dma((chunks, 3)),
            dma((chunks, n_t)),
            dma,
        ],
        compiler_params=pltpu.CompilerParams(
            collective_id=0, has_side_effects=True, vmem_limit_bytes=56 << 20
        ),
    )(
        queries, key_rows, value_rows, w_out, residual,
        out_gate.reshape(1, out_cols), coef, q_feat, k_feat,
    )


def solution(mesh):
    placed = (
        P("seq", "tensor"),
        P(("seq", "tensor"), None),
        P(("seq", "tensor"), None),
        P(("seq", "tensor"), None),
        P(None, "tensor"),
        P("tensor"),
        P(),
    )
    return jax.shard_map(
        shards, mesh=mesh, in_specs=placed, out_specs=P("seq", "tensor"), check_vma=False
    )
```

time: 311 us -> 91.4 us (0.29)
  waiting for transfers between devices: 149 us -> 0 us
  Pallas kernels: 0 us -> 84.4 us
  matrix products: 51.5 us -> 0 us
  local copies, waits for them, and re-layouts: 54.1 us -> 5.85 us
  other arithmetic: 22.3 us -> 0.08 us
  starting transfers between devices: 18.2 us -> 0 us
  between operations: 13.6 us -> 0.02 us
    pallas_call x0 -> x1, Pallas kernels: none -> 84.4 us  [shards(): pl.pallas_call(functools.partial(kernel, n_t, n_s, frames), out_shape=jax...]
    ppermute x2 -> x0, waiting for transfers between devices: 80.9 us -> none  [passed_along(): return lax.ppermute(value, axis, pairs)]
    dot_general x5 -> x0, matrix products: 51.5 us -> none  [the longest x3 24.5 us: part_scores(): jnp.einsum('qhd,khd->hqk', query_tiles, key_tiles, preferred_element_type...]
    all_gather x1 -> x0, waiting for transfers between devices: 38.6 us -> none  [shards(): lax.all_gather(head_out, 'tensor', axis=1, tiled=True)]
    concatenate x4 -> x1, local copies, waits for them, and re-layouts: 36.8 us -> 0.68 us  [shards(): jnp.concatenate([jnp.ones((heads_here, 8), jnp.float32), jnp.repeat(stops...]
    all_to_all x3 -> x0, waiting for transfers between devices: 29.2 us -> none  [the longest x1 13.9 us: shards(): lax.all_to_all(key_rows, 'tensor', split_axis=1, concat_axis=0, tiled=True)]
    reduce_sum x1 -> x0, other arithmetic: 14.1 us -> none  [shards(): row_sum = jnp.sum(exp_scores, axis=-1, keepdims=True)]
    all_to_all x3 -> x0, starting transfers between devices: 12.9 us -> none  [the longest x1 4.37 us: shards(): lax.all_to_all(value_rows, 'tensor', split_axis=1, concat_axis=0, tiled=T...]
  transfers between devices with their start and end apart: 6 -> 0, of which waited for: 5 -> 0; matrix products, arithmetic and copies ran while one was open for 7% -> 0% of each run, Pallas kernels for 0% -> 0%
where the time goes in v1:
time: 91.4 us; the launch traced here: 90.3 us
  Pallas kernels  84.4 us (92%)
  local copies, waits for them, and re-layouts  5.85 us (6%)
    pallas_call x1, Pallas kernels, shards(): pl.pallas_call(functools.partial(kernel, n_t, n_s, frames), out_shape=jax...  84.4 us
    unnamed x4, local copies, waits for them, and re-layouts  3.49 us

profile of v1, /device:TPU:9, one launch (start us, length us, event | category | flops | bytes accessed | tf_op | source)
XLA Modules:
  0.0 90.3 jit_solution(9736925291029789906)
XLA Ops:
  0.0 0.0 copy-start
  0.0 0.1 add_convert_fusion
  0.1 0.6 copy-done
  0.7 0.1 constant_dynamic-slice_fusion
  0.8 0.1 copy.12
  0.8 0.2 slice_reduce_fusion
  1.0 0.1 reshape.33
  1.1 0.1 reshape.32
  1.2 0.7 concatenate.7
  1.8 1.3 %reshape.31.gate_ref = f32[1,1536]{1,0:T(1,128)} reshape(f32[1536]{0:T(1024)} %param.14) | data formatting | bytes 12288 | tf_op jit(solution)/shard_map/reshape | solution.py:447
  3.1 84.4 %shard_map.91 = bf16[576,1536]{1,0:T(8,128)(2,1)} custom-call(bf16[144,4096]{1,0:T(8,128)(2,1)} %q_hbm.1, bf16[144,4096]{1,0:T(8,128)(2,1)} %k_hbm.1, bf16[144,4096]{1,0:T(8,128)(2,1)} %v_hbm.1, bf16[4096,1536]{1,0:T(8,128)(2,1)} %w_hbm.1, bf16[576,1536]{1,0:T(8,128)(2,1)} %res_hbm.1, f32[1,1536]{1,0:T(1,128)} %reshape.31.gate_ref, f32[8,1,128]{2,1,0:T(1,128)} %bitcast.3, ...), custom_call_target="tpu_custom_call" | custom-call | tf_op jit(solution)/shard_map/pallas_call | solution.py:420
  87.5 2.8 %copy.14 = bf16[576,1536]{1,0:T(8,128)(2,1)} copy(bf16[576,1536]{1,0:T(8,128)(2,1)} %shard_map.91) | data formatting | bytes 3538944
  (4 shorter events, 0.0 us)
Async XLA Ops:
  0.0 0.7 copy-start

commit v2 on v1

--- a/solution.py
+++ b/solution.py
@@ -14,6 +14,7 @@
 HT_DEV = 2
 WT = 3
 CHUNK_HEADS = 2
+OUT_TILE = 512
 FAR = -1e30
 MESH = pl.DeviceIdType.MESH
 
@@ -126,9 +127,9 @@
 
 
 def kernel(
-    n_t, n_s, frames, q_hbm, k_hbm, v_hbm, w_hbm, res_hbm, gate_ref, coef_ref, qf_ref, kf_ref,
-    out_ref, own, halo, gat, wbuf, res, acc,
-    a_send, a_recv, a_loc, h_send, h_recv, g_send, g_recv, w_sem, r_sem,
+    n_t, n_s, frames, q_hbm, k_hbm, v_hbm, w_hbm, res_hbm, qf_hbm, kf_hbm, gate_ref, ext_ref,
+    out_hbm, own, halo, gat, wbuf, res, acc, out, qf, kf,
+    a_send, a_recv, a_loc, h_send, h_recv, g_send, g_recv, w_sem, c_sem, o_sem,
 ):
     rows = q_hbm.shape[0]
     inner_dev = q_hbm.shape[1] // n_t
@@ -203,24 +204,24 @@
             device_id_type=MESH,
         )
 
-    def shared(c, kind):
+    def shared(c, h, kind):
         piece = across if kind == 2 else me
         return pltpu.make_async_remote_copy(
-            src_ref=gat.at[c, piece],
-            dst_ref=gat.at[c, piece],
-            send_sem=g_send.at[c, kind],
-            recv_sem=g_recv.at[c, kind],
+            src_ref=gat.at[c, h, piece],
+            dst_ref=gat.at[c, h, piece],
+            send_sem=g_send.at[c, h, kind],
+            recv_sem=g_recv.at[c, h, kind],
             device_id={"tensor": across if kind == 1 else mate},
             device_id_type=MESH,
         )
 
-    def shared_in(c, kind):
+    def shared_in(c, h, kind):
         piece = (mate, across, lax.rem(mate + n_t // 2, n_t))[kind]
         return pltpu.make_async_remote_copy(
-            src_ref=gat.at[c, piece],
-            dst_ref=gat.at[c, piece],
-            send_sem=g_send.at[c, kind],
-            recv_sem=g_recv.at[c, kind],
+            src_ref=gat.at[c, h, piece],
+            dst_ref=gat.at[c, h, piece],
+            send_sem=g_send.at[c, h, kind],
+            recv_sem=g_recv.at[c, h, kind],
             device_id={"tensor": across if kind == 1 else mate},
             device_id_type=MESH,
         )
@@ -244,8 +245,12 @@
         for s in range(n_t):
             weights_in(c, s).start()
 
-    res_copy = pltpu.make_async_copy(res_hbm, res, r_sem)
-    res_copy.start()
+    consts = [
+        pltpu.make_async_copy(src, dst, c_sem.at[i])
+        for i, (src, dst) in enumerate(((qf_hbm, qf), (kf_hbm, kf), (res_hbm, res)))
+    ]
+    for copy in consts:
+        copy.start()
     acc[...] = jnp.zeros_like(acc)
 
     @pl.when(sb == 0)
@@ -278,6 +283,16 @@
             parts += [far, near] if r == 0 else [near, far]
         return jnp.concatenate(parts, axis=0)
 
+    def switches(head):
+        lane = lax.broadcasted_iota(jnp.int32, (1, HEAD_DIM), 1)
+        at = me * (inner_dev // HEAD_DIM) + head
+        coef = jnp.where(lane < 8, 1.0, 0.0)
+        for d, first, last in ((0, 8, 11), (2, 11, 14), (1, 14, 15)):
+            stop = (1 - ext_ref[d, at]).astype(jnp.float32)
+            coef = jnp.where((lane >= first) & (lane < last), stop, coef)
+        coef = jnp.where(lane == 15, jnp.where(sb == 0, 1.0, 0.0), coef)
+        return jnp.where(lane == 16, jnp.where(sb == n_s - 1, 1.0, 0.0), coef)
+
     def attend(c):
         arrived(2, c)
         for a in range(2):
@@ -295,15 +310,15 @@
         ones = jnp.ones((frames * 3 * span, HEAD_DIM), jnp.bfloat16)
         for h in range(CHUNK_HEADS):
             lanes = slice(h * HEAD_DIM, (h + 1) * HEAD_DIM)
-            coef = coef_ref[c * CHUNK_HEADS + h]
+            coef = switches(c * CHUNK_HEADS + h)
             for r in range(2):
                 q_part = jnp.concatenate(
                     [own[2, c, (2 * f + r) * span : (2 * f + r + 1) * span, lanes]
                      for f in range(frames)], axis=0)
-                q_feat = (qf_ref[r].astype(jnp.float32) * coef).astype(jnp.bfloat16)
+                q_feat = (qf[r].astype(jnp.float32) * coef).astype(jnp.bfloat16)
                 scores = lax.dot_general(
                     jnp.concatenate([q_part, q_feat], axis=1),
-                    jnp.concatenate([gathered(0, c, r, lanes), kf_ref[r]], axis=1),
+                    jnp.concatenate([gathered(0, c, r, lanes), kf[r]], axis=1),
                     (((1,), (1,)), ((), ())),
                     preferred_element_type=jnp.float32,
                 )
@@ -318,29 +333,28 @@
                 )
                 done = (both[:, :HEAD_DIM] / both[:, HEAD_DIM:]).astype(jnp.bfloat16)
                 for f in range(frames):
-                    gat[c, me, (2 * f + r) * span : (2 * f + r + 1) * span, lanes] = done[
+                    gat[c, h, me, (2 * f + r) * span : (2 * f + r + 1) * span] = done[
                         f * span : (f + 1) * span
                     ]
-        shared(c, 1).start()
-        shared(c, 0).start()
-
-    n_tile = 512
-
-    def project(c):
-        shared_in(c, 0).wait_recv()
-        shared_in(c, 2).wait_recv()
+            shared(c, h, 1).start()
+            shared(c, h, 0).start()
+
+    def gathered_in(c):
+        for h in range(CHUNK_HEADS):
+            shared_in(c, h, 0).wait_recv()
+            shared_in(c, h, 2).wait_recv()
         for s in range(n_t):
             weights_in(c, s).wait()
 
-        @pl.loop(0, acc.shape[1] // n_tile)
-        def _(j):
-            cols = pl.ds(pl.multiple_of(j * n_tile, n_tile), n_tile)
-            lhs = jnp.concatenate([gat[c, s] for s in range(n_t)], axis=1)
-            acc[:, cols] += jnp.dot(lhs, wbuf[c, :, cols], preferred_element_type=jnp.float32)
-
+    def project(c, cols):
+        lhs = jnp.concatenate([gat[c, h, s] for s in range(n_t) for h in range(CHUNK_HEADS)], axis=1)
+        return acc[:, cols] + jnp.dot(lhs, wbuf[c, :, cols], preferred_element_type=jnp.float32)
+
+    consts[0].wait()
+    consts[1].wait()
     halo_start(0)
 
-    @pl.loop(0, chunks + 2)
+    @pl.loop(0, chunks + 1)
     def _(s):
         @pl.when(s + 1 < chunks)
         def _():
@@ -348,19 +362,34 @@
 
         @pl.when(s >= 2)
         def _():
-            project(s - 2)
-
-        @pl.when((s >= 1) & (s <= chunks))
+            gathered_in(s - 2)
+
+            @pl.loop(0, acc.shape[1] // OUT_TILE)
+            def _(j):
+                cols = pl.ds(pl.multiple_of(j * OUT_TILE, OUT_TILE), OUT_TILE)
+                acc[:, cols] = project(s - 2, cols)
+
+        @pl.when(s >= 1)
         def _():
-            shared_in(s - 1, 1).wait_recv()
-            shared(s - 1, 2).start()
+            for h in range(CHUNK_HEADS):
+                shared_in(s - 1, h, 1).wait_recv()
+                shared(s - 1, h, 2).start()
 
         @pl.when(s < chunks)
         def _():
             attend(s)
 
-    res_copy.wait()
-    out_ref[...] = (res[...].astype(jnp.float32) + gate_ref[...] * acc[...]).astype(out_ref.dtype)
+    consts[2].wait()
+    gathered_in(chunks - 1)
+    written = []
+    for j in range(acc.shape[1] // OUT_TILE):
+        cols = slice(j * OUT_TILE, (j + 1) * OUT_TILE)
+        gate = gate_ref[cols].reshape(1, OUT_TILE)
+        total = project(chunks - 1, cols)
+        out[:, cols] = (res[:, cols].astype(jnp.float32) + gate * total).astype(out.dtype)
+        copy = pltpu.make_async_copy(out.at[:, cols], out_hbm.at[:, cols], o_sem.at[j])
+        copy.start()
+        written.append(copy)
 
     @pl.loop(0, chunks)
     def _(c):
@@ -380,7 +409,11 @@
                     edge(1, a, c, f).wait_send()
 
         for kind in range(3):
-            shared(c, kind).wait_send()
+            for h in range(CHUNK_HEADS):
+                shared(c, h, kind).wait_send()
+
+    for copy in written:
+        copy.wait()
 
 
 def shards(residual, queries, key_rows, value_rows, w_out, out_gate, extents):
@@ -389,29 +422,13 @@
     tokens, out_cols = residual.shape
     inner_dev = inner // n_t
     width = CHUNK_HEADS * HEAD_DIM
-    if n_t != 4 or n_s < 2 or rows % 16 or inner_dev % width or out_cols % 512:
+    if n_t != 4 or n_s < 2 or rows % 16 or inner_dev % width or out_cols % OUT_TILE:
         return plain_shards(
             residual, queries, key_rows, value_rows, w_out, out_gate, extents
         )
-    heads_here = inner_dev // HEAD_DIM
     chunks = inner_dev // width
     frames = tokens // (HT_DEV * WT * TILE)
     half = tokens // HT_DEV
-    reach = lax.dynamic_slice_in_dim(extents, lax.axis_index("tensor") * heads_here, heads_here, 0)
-    stops = (reach < 1).astype(jnp.float32)
-    sb = lax.axis_index("seq")
-    at_edge = jnp.stack([sb == 0, sb == n_s - 1]).astype(jnp.float32)
-    coef = jnp.concatenate(
-        [
-            jnp.ones((heads_here, 8), jnp.float32),
-            jnp.repeat(stops[:, 0:1], 3, axis=1),
-            jnp.repeat(stops[:, 2:3], 3, axis=1),
-            stops[:, 1:2],
-            jnp.broadcast_to(at_edge[None], (heads_here, 2)),
-            jnp.zeros((heads_here, HEAD_DIM - 17), jnp.float32),
-        ],
-        axis=1,
-    ).reshape(heads_here, 1, HEAD_DIM)
     q_feat, k_feat = mask_features(frames)
     hbm = pl.BlockSpec(memory_space=pl.ANY)
     vmem = pl.BlockSpec(memory_space=pltpu.VMEM)
@@ -420,31 +437,34 @@
     return pl.pallas_call(
         functools.partial(kernel, n_t, n_s, frames),
         out_shape=jax.ShapeDtypeStruct((tokens, out_cols), bf16),
-        in_specs=[hbm] * 5 + [vmem] * 4,
-        out_specs=vmem,
+        in_specs=[hbm] * 7 + [vmem, pl.BlockSpec(memory_space=pltpu.SMEM)],
+        out_specs=hbm,
         scratch_shapes=[
             pltpu.VMEM((3, chunks, tokens, width), bf16),
             pltpu.VMEM((2, 2, chunks, half, width), bf16),
-            pltpu.VMEM((chunks, n_t, tokens, width), bf16),
+            pltpu.VMEM((chunks, CHUNK_HEADS, n_t, tokens, HEAD_DIM), bf16),
             pltpu.VMEM((chunks, n_t * width, out_cols), bf16),
             pltpu.VMEM((tokens, out_cols), bf16),
             pltpu.VMEM((tokens, out_cols), jnp.float32),
+            pltpu.VMEM((tokens, out_cols), bf16),
+            pltpu.VMEM(q_feat.shape, bf16),
+            pltpu.VMEM(k_feat.shape, bf16),
             dma((3, chunks, n_t - 1)),
             dma((3, chunks, n_t - 1)),
             dma((3, chunks)),
             dma((2, 2, chunks, frames)),
             dma((2, 2, chunks, frames)),
-            dma((chunks, 3)),
-            dma((chunks, 3)),
+            dma((chunks, CHUNK_HEADS, 3)),
+            dma((chunks, CHUNK_HEADS, 3)),
             dma((chunks, n_t)),
-            dma,
+            dma((3,)),
+            dma((out_cols // OUT_TILE,)),
         ],
         compiler_params=pltpu.CompilerParams(
             collective_id=0, has_side_effects=True, vmem_limit_bytes=56 << 20
         ),
     )(
-        queries, key_rows, value_rows, w_out, residual,
-        out_gate.reshape(1, out_cols), coef, q_feat, k_feat,
+        queries, key_rows, value_rows, w_out, residual, q_feat, k_feat, out_gate, extents.T,
     )
 
 

time: 91.4 us -> 84.9 us (0.929)
  local copies, waits for them, and re-layouts: 5.85 us -> 2.8 us
  Pallas kernels: 84.4 us -> 81.9 us
    pallas_call x1, Pallas kernels: 84.4 us -> 81.9 us  [shards(): pl.pallas_call(functools.partial(kernel, n_t, n_s, frames), out_shape=jax...]
    reshape x3 -> x0, local copies, waits for them, and re-layouts: 1.43 us -> none  [the longest x1 1.29 us: shards(): out_gate.reshape(1, out_cols)]
    unnamed x4 -> x1, local copies, waits for them, and re-layouts: 3.49 us -> 2.8 us
where the time goes in v2:
time: 84.9 us; the launch traced here: 84.7 us
  Pallas kernels  81.9 us (96%)
  local copies, waits for them, and re-layouts  2.8 us (3%)
    pallas_call x1, Pallas kernels, shards(): pl.pallas_call(functools.partial(kernel, n_t, n_s, frames), out_shape=jax...  81.9 us
    unnamed x1, local copies, waits for them, and re-layouts  2.8 us

profile of v2, /device:TPU:9, one launch (start us, length us, event | category | flops | bytes accessed | tf_op | source)
XLA Modules:
  0.0 84.7 jit_solution(10664003007442468717)
XLA Ops:
  0.0 81.9 %shard_map.91 = bf16[576,1536]{1,0:T(8,128)(2,1)} custom-call(bf16[144,4096]{1,0:T(8,128)(2,1)} %q_hbm.1, bf16[144,4096]{1,0:T(8,128)(2,1)} %k_hbm.1, bf16[144,4096]{1,0:T(8,128)(2,1)} %v_hbm.1, bf16[4096,1536]{1,0:T(8,128)(2,1)} %w_hbm.1, bf16[576,1536]{1,0:T(8,128)(2,1)} %res_hbm.1, bf16[2,288,128]{2,1,0:T(8,128)(2,1)} %constant.4.clone.qf_hbm, ...), custom_call_target="tpu_custom_call" | custom-call | tf_op jit(solution)/shard_map/pallas_call | solution.py:437
  81.9 2.8 %copy.11 = bf16[576,1536]{1,0:T(8,128)(2,1)} copy(bf16[576,1536]{1,0:T(8,128)(2,1)} %shard_map.91) | data formatting | bytes 3538944

commit v3 on v2

--- a/solution.py
+++ b/solution.py
@@ -354,30 +354,46 @@
     consts[1].wait()
     halo_start(0)
 
-    @pl.loop(0, chunks + 1)
+    def forward(c):
+        for h in range(CHUNK_HEADS):
+            shared_in(c, h, 1).wait_recv()
+            shared(c, h, 2).start()
+
+    def accumulate(c):
+        gathered_in(c)
+
+        @pl.loop(0, acc.shape[1] // OUT_TILE)
+        def _(j):
+            cols = pl.ds(pl.multiple_of(j * OUT_TILE, OUT_TILE), OUT_TILE)
+            acc[:, cols] = project(c, cols)
+
+    early = chunks - 2
+
+    @pl.loop(0, chunks)
     def _(s):
         @pl.when(s + 1 < chunks)
         def _():
             halo_start(s + 1)
 
-        @pl.when(s >= 2)
+        @pl.when(s == chunks - 1)
         def _():
-            gathered_in(s - 2)
-
-            @pl.loop(0, acc.shape[1] // OUT_TILE)
-            def _(j):
-                cols = pl.ds(pl.multiple_of(j * OUT_TILE, OUT_TILE), OUT_TILE)
-                acc[:, cols] = project(s - 2, cols)
-
-        @pl.when(s >= 1)
+            @pl.loop(0, early)
+            def _(c):
+                @pl.when(c >= 1)
+                def _():
+                    accumulate(c - 1)
+
+                forward(c)
+
+        attend(s)
+
+    @pl.loop(early, chunks)
+    def _(c):
+        @pl.when(c >= 1)
         def _():
-            for h in range(CHUNK_HEADS):
-                shared_in(s - 1, h, 1).wait_recv()
-                shared(s - 1, h, 2).start()
-
-        @pl.when(s < chunks)
-        def _():
-            attend(s)
+            accumulate(c - 1)
+
+        forward(c)
 
     consts[2].wait()
     gathered_in(chunks - 1)

time: 84.9 us -> 80.4 us (0.947)
  Pallas kernels: 81.9 us -> 77.4 us
    pallas_call x1, Pallas kernels: 81.9 us -> 77.4 us  [shards(): pl.pallas_call(functools.partial(kernel, n_t, n_s, frames), out_shape=jax...]
where the time goes in v3:
time: 80.4 us; the launch traced here: 80.2 us
  Pallas kernels  77.4 us (96%)
  local copies, waits for them, and re-layouts  2.8 us (3%)
    pallas_call x1, Pallas kernels, shards(): pl.pallas_call(functools.partial(kernel, n_t, n_s, frames), out_shape=jax...  77.4 us
    unnamed x1, local copies, waits for them, and re-layouts  2.8 us

profile of v3, /device:TPU:9, one launch (start us, length us, event | category | flops | bytes accessed | tf_op | source)
XLA Modules:
  0.0 80.2 jit_solution(15659706645492565795)
XLA Ops:
  0.0 77.4 %shard_map.91 = bf16[576,1536]{1,0:T(8,128)(2,1)} custom-call(bf16[144,4096]{1,0:T(8,128)(2,1)} %q_hbm.1, bf16[144,4096]{1,0:T(8,128)(2,1)} %k_hbm.1, bf16[144,4096]{1,0:T(8,128)(2,1)} %v_hbm.1, bf16[4096,1536]{1,0:T(8,128)(2,1)} %w_hbm.1, bf16[576,1536]{1,0:T(8,128)(2,1)} %res_hbm.1, bf16[2,288,128]{2,1,0:T(8,128)(2,1)} %constant.4.clone.qf_hbm, ...), custom_call_target="tpu_custom_call" | custom-call | tf_op jit(solution)/shard_map/pallas_call | solution.py:453
  77.4 2.8 %copy.11 = bf16[576,1536]{1,0:T(8,128)(2,1)} copy(bf16[576,1536]{1,0:T(8,128)(2,1)} %shard_map.91) | data formatting | bytes 3538944
